TPU v7x, 128 devices: a whole 4x4x4 slice. The times are simulated.
128 devices in a mesh: facet: 8 (over y, core), sub: 16 (over z, x).
Axes of the slice: x: 4, y: 4, z: 4, core: 2. Of those that a mesh axis runs over, the one named last changes fastest.
Arguments:
- facet_data: bfloat16 [2, 16, 65536], P(None, None, ('facet', 'sub')), may hold values from -6 to 6
- subgrid_pos: int32 [128], P(('facet', 'sub')), may hold values from 0 to 65408, as said below
- vis_counts: int32 [128], P(('facet', 'sub')), may hold values from 128 to 512, as said below
- vis_u_fine: int32 [128, 512], P(('facet', 'sub')), may hold values from 0 to 8079
- vis_v_fine: int32 [128, 512], P(('facet', 'sub')), may hold values from 0 to 143
- vis_observed: float32 [2, 128, 512], P(None, ('facet', 'sub')), may hold values from -6 to 6
Outputs:
- vis_residual: float32 [2, 128, 512], P(None, ('facet', 'sub'))
- facet_residual: float32 [2, 16, 65536], P(None, None, ('facet', 'sub'))
Inputs may be any that keep to these rules, and one draw needn't show every extreme that they name: `subgrid_pos`: distinct multiples of 128; a subgrid's u cells o to o + 511 are taken modulo 65536. The first vis_counts[s] slots of subgrid s are live; some subgrid has all 512 slots live.
All inputs are finite; a program needn't handle non-finite values.
Results may differ from a plain program's by a relative error of at most 0.012.
Values may be sent and summed in bfloat16 or wider, within the bound.
No kernel may reach another device: no remote copies, remote signals or barrier semaphores. Data moves between devices by JAX's collectives and lax.ppermute only.
A program may use at most 64 MiB of HBM per device.

v0:
```python
import math

import jax
import jax.numpy as jnp
from jax import lax
from jax.sharding import PartitionSpec as P

FW = 8192
SG = 512
KS = 8
OVER = 16


def phase_slot_index(left_side, right_side, image_width):
    right_high = right_side // 256
    right_low = right_side % 256
    return (
        left_side * right_low % image_width + left_side * right_high % image_width * 256
    ) % image_width


def phasor(phase_total_count, image_width):
    phase_angle = 2.0 * math.pi * (phase_total_count.astype(jnp.float32) / float(image_width))
    return (jnp.cos(phase_angle), jnp.sin(phase_angle))


def build_phase_tables(sub_width, image_width):
    table_range = jnp.arange(sub_width, dtype=jnp.int32)
    cosine, sine_part = phasor(
        phase_slot_index(table_range[:, None], table_range[None, :], image_width), image_width
    )
    norm_scale = 1.0 / math.sqrt(image_width)
    real_part = (cosine * norm_scale).astype(jnp.bfloat16)
    imag_part = (-sine_part * norm_scale).astype(jnp.bfloat16)
    forward_table = jnp.concatenate(
        [jnp.concatenate([real_part, imag_part], 1), jnp.concatenate([-imag_part, real_part], 1)], 0
    )
    backward_table = jnp.concatenate(
        [jnp.concatenate([real_part, -imag_part], 1), jnp.concatenate([imag_part, real_part], 1)], 0
    )
    return (forward_table, backward_table)


def forward_part(columns, x_start, positions, table, image_width):
    sub_width = table.shape[0] // 2
    rows_v = columns.shape[1]
    blocks = columns.shape[2] // sub_width
    inside = jnp.arange(sub_width, dtype=jnp.int32)
    mod_cos, mod_sin = phasor(
        phase_slot_index(inside[None, :], positions[:, None], image_width), image_width
    )
    mod_cos = mod_cos[:, None, None, :]
    mod_sin = mod_sin[:, None, None, :]
    image_band = columns.astype(jnp.float32).reshape(2, rows_v, blocks, sub_width)
    real_z = image_band[0][None] * mod_cos + image_band[1][None] * mod_sin
    imag_z = image_band[1][None] * mod_cos - image_band[0][None] * mod_sin
    stacked = jnp.concatenate([real_z, imag_z], -1).astype(jnp.bfloat16)
    partial_grid = jnp.dot(stacked, table, preferred_element_type=jnp.float32)
    anchors = x_start + jnp.arange(blocks, dtype=jnp.int32) * sub_width
    columns_u = (positions[:, None] + inside[None, :]) % image_width
    post_cos, post_sin = phasor(
        phase_slot_index(anchors[None, :, None], columns_u[:, None, :], image_width), image_width
    )
    post_cos = post_cos[:, None]
    post_sin = post_sin[:, None]
    real_p = partial_grid[..., :sub_width]
    imag_p = partial_grid[..., sub_width:]
    real_g = jnp.sum(real_p * post_cos + imag_p * post_sin, axis=2)
    imag_g = jnp.sum(imag_p * post_cos - real_p * post_sin, axis=2)
    return jnp.concatenate([real_g, imag_g], -1)


def kernel_weights(fine_index, cells):
    cell_index = fine_index // OVER
    frac_index = fine_index % OVER
    cell_range = jnp.arange(cells, dtype=jnp.int32)
    cell_offset = cell_range[None, None, :] - cell_index[..., None]
    distance = (
        cell_offset.astype(jnp.float32)
        - (KS - 1) / 2.0
        - frac_index.astype(jnp.float32)[..., None] / OVER
    )
    weight = jnp.exp(-0.5 * (distance / 0.6) ** 2)
    return jnp.where((cell_offset >= 0) & (cell_offset < KS), weight, jnp.float32(0.0))


def degrid_regrid(subgrid_data, u_fine, v_fine, counts, observed):
    sub_width = subgrid_data.shape[2] // 2
    weight_u = kernel_weights(u_fine, sub_width)
    kernel_weight_v = kernel_weights(v_fine, subgrid_data.shape[1])
    gridded_values = subgrid_data.astype(jnp.float32)
    along_v_axis = jnp.einsum(
        "jtz,jzh->jth", kernel_weight_v, gridded_values, precision=lax.Precision.HIGHEST
    )
    real_pred = jnp.sum(along_v_axis[..., :sub_width] * weight_u, -1)
    imag_pred = jnp.sum(along_v_axis[..., sub_width:] * weight_u, -1)
    slot_range = jnp.arange(u_fine.shape[1], dtype=jnp.int32)
    live_mask = slot_range[None, :] < counts[:, None]
    real_res = jnp.where(live_mask, observed[0] - real_pred, jnp.float32(0.0))
    imag_res = jnp.where(live_mask, observed[1] - imag_pred, jnp.float32(0.0))
    spread_onto_grid = jnp.concatenate(
        [real_res[..., None] * weight_u, imag_res[..., None] * weight_u], -1
    )
    regridded_values = jnp.einsum(
        "mlz,mlr->mzr", kernel_weight_v, spread_onto_grid, precision=lax.Precision.HIGHEST
    ).astype(jnp.bfloat16)
    return (jnp.stack([real_res, imag_res]), regridded_values)


def backward_part(grids, positions, x_start, span, table, image_width):
    sub_width = table.shape[0] // 2
    rows_v = grids.shape[1]
    blocks = span // sub_width
    inside = jnp.arange(sub_width, dtype=jnp.int32)
    anchors = x_start + jnp.arange(blocks, dtype=jnp.int32) * sub_width
    columns_u = (positions[:, None] + inside[None, :]) % image_width
    pre_cos, pre_sin = phasor(
        phase_slot_index(anchors[None, :, None], columns_u[:, None, :], image_width), image_width
    )
    pre_cos = pre_cos[:, None]
    pre_sin = pre_sin[:, None]
    real_h = grids[..., :sub_width].astype(jnp.float32)[:, :, None, :]
    imag_h = grids[..., sub_width:].astype(jnp.float32)[:, :, None, :]
    real_m = real_h * pre_cos - imag_h * pre_sin
    imag_m = real_h * pre_sin + imag_h * pre_cos
    stacked = jnp.concatenate([real_m, imag_m], -1).astype(jnp.bfloat16)
    product = jnp.dot(stacked, table, preferred_element_type=jnp.float32)
    mod_cos, mod_sin = phasor(
        phase_slot_index(inside[None, :], positions[:, None], image_width), image_width
    )
    mod_cos = mod_cos[:, None, None, :]
    mod_sin = mod_sin[:, None, None, :]
    real_q = product[..., :sub_width]
    imag_q = product[..., sub_width:]
    real_out = jnp.sum(real_q * mod_cos - imag_q * mod_sin, axis=0)
    imag_out = jnp.sum(real_q * mod_sin + imag_q * mod_cos, axis=0)
    return jnp.stack([real_out, imag_out]).reshape(2, rows_v, span)


def shards(facet_data, subgrid_pos, vis_counts, vis_u_fine, vis_v_fine, vis_observed):
    facets = lax.axis_size("facet")
    sub_count = lax.axis_size("sub")
    image_width = FW * facets
    columns = facet_data.shape[2]
    device_place = lax.axis_index("facet") * sub_count + lax.axis_index("sub")
    x_begin = device_place * columns
    forward_table, backward_table = build_phase_tables(SG, image_width)
    every_spot = lax.all_gather(subgrid_pos, ("facet", "sub"), axis=0, tiled=True)
    summed = lax.psum_scatter(
        forward_part(facet_data, x_begin, every_spot, forward_table, image_width),
        ("facet", "sub"),
        scatter_dimension=0,
        tiled=True,
    )
    subgrid_data = summed.astype(jnp.bfloat16)
    residual, regridded_values = degrid_regrid(
        subgrid_data, vis_u_fine, vis_v_fine, vis_counts, vis_observed
    )
    residual_image = backward_part(
        lax.all_gather(regridded_values, ("facet", "sub"), axis=0, tiled=True),
        lax.all_gather(subgrid_pos, ("facet", "sub"), axis=0, tiled=True),
        x_begin,
        columns,
        backward_table,
        image_width,
    )
    return (residual, residual_image)


def solution(mesh):
    return jax.shard_map(
        shards,
        mesh=mesh,
        in_specs=(
            P(None, None, ("facet", "sub")),
            P(("facet", "sub")),
            P(("facet", "sub")),
            P(("facet", "sub"), None),
            P(("facet", "sub"), None),
            P(None, ("facet", "sub"), None),
        ),
        out_specs=(P(None, ("facet", "sub"), None), P(None, None, ("facet", "sub"))),
        check_vma=False,
    )
```

profile of v0, /device:TPU:1, one launch (start us, length us, event | category | flops | bytes accessed | tf_op | source)
XLA Modules:
  0.0 855.2 jit_solution(13696291274715392463)
XLA Ops:
  7.2 5.2 multiply_convert_fusion
  12.5 4.9 fusion.78
  18.0 0.1 dynamic-update-slice
  18.1 68.6 %all-reduce = s32[128]{0:T(128)S(1)} all-reduce(s32[128]{0:T(128)S(1)} %dynamic-update-slice), channel_id=1, replica_groups=mesh['facet'=8,'sub'=16] {'facet','sub'}, use_global_device_ids=true, to_apply=%add | all-reduce | flops 128 | bytes 1024
  86.8 0.8 convert_element_type.123
  87.6 1.6 fusion.75
  89.2 1.3 fusion.77
  90.6 1.3 add_convert_fusion
  91.9 4.5 fusion.15
  96.5 3.1 add_bitcast_fusion
  99.5 3.2 pad_maximum_fusion
  102.8 8.3 copy.15
  111.9 626.0 %reduce-scatter.2.cloned.1.call-done = f32[1,16,1024]{2,1,0:T(8,128)} async-done(((f32[128,16,1024]{2,1,0:T(8,128)}), f32[1,16,1024]{2,1,0:T(8,128)}) %reduce-scatter.2.cloned.1.call-update) | async-done | bytes 65552 | tf_op jit(solution)/shard_map/reduce_scatter | solution.py:149
  737.9 1.9 convolution_bitcast_fusion
  739.8 0.8 fusion.42
  740.6 0.6 broadcast_multiply_fusion.1
  741.3 1.8 fusion.33
  743.1 0.6 pad_maximum_fusion.7
  743.7 92.4 %all-gather.3.cloned.1.call-done = bf16[2048,1024]{1,0:T(8,128)(2,1)} async-done(((bf16[16,1024]{1,0:T(8,128)(2,1)}), bf16[2048,1024]{1,0:T(8,128)(2,1)}) %all-gather.3.cloned.1.call-update) | async-done | bytes 4194320 | tf_op jit(solution)/shard_map/all_gather | solution.py:160
  836.1 2.7 fusion.124
  838.8 3.0 fusion.1
  841.9 4.5 fusion.12
  846.5 1.3 subtract_reduce_fusion
  847.7 0.6 maximum_bitcast_fusion.4
  (49 shorter events, 0.3 us)
Async XLA Ops:
  7.2 730.7 %reduce-scatter.2.cloned.1.call-start = ((), (), s32[]{:S(2)}) async-start(), calls=%async_computation.1 | async-start | bytes 8454144 | tf_op jit(solution)/shard_map/reduce_scatter | solution.py:149
  12.4 84.0 %copy-start.8 = (bf16[512,512]{1,0:T(8,128)(2,1)}, bf16[512,512]{1,0:T(8,128)(2,1)S(1)}, u32[]{:S(2)}) copy-start(bf16[512,512]{1,0:T(8,128)(2,1)S(1)} %get-tuple-element.26) | copy-start | bytes 1572868
  12.5 84.0 %copy-start.10 = (bf16[512,512]{1,0:T(8,128)(2,1)}, bf16[512,512]{1,0:T(8,128)(2,1)S(1)}, u32[]{:S(2)}) copy-start(bf16[512,512]{1,0:T(8,128)(2,1)S(1)} %get-tuple-element.27) | copy-start | bytes 1572868
  17.3 79.1 %copy-start.12 = (bf16[512,512]{1,0:T(8,128)(2,1)}, bf16[512,512]{1,0:T(8,128)(2,1)S(1)}, u32[]{:S(2)}) copy-start(bf16[512,512]{1,0:T(8,128)(2,1)S(1)} %fusion.78) | copy-start | bytes 1572868
  89.2 7.3 copy-start
  89.2 7.3 copy-start.2
  90.5 1.3 copy-start.4
  90.6 1.3 copy-start.6
  111.1 0.7 copy-start.15
  111.1 0.8 copy-start.16
  111.1 629.4 %copy-start.14 = (f32[2,1,512]{2,1,0:T(1,128)S(1)}, f32[2,1,512]{2,1,0:T(1,128)}, u32[]{:S(2)}) copy-start(f32[2,1,512]{2,1,0:T(1,128)} %param.11) | copy-start | bytes 12292
  111.2 724.9 %all-gather.3.cloned.1.call-start = ((), (), s32[]{:S(2)}) async-start(), calls=%async_computation.2 | async-start | bytes 4227072 | tf_op jit(solution)/shard_map/all_gather | solution.py:160
  836.1 2.7 copy-start.1
  836.1 2.7 copy-start.3
  838.8 3.1 copy-start.9
  838.8 3.1 copy-start.11
  838.8 3.1 copy-start.13
  841.9 4.6 copy-start.5
  841.9 4.6 copy-start.7
Sparse Core Ops, SparseCore 0:
  111.3 626.5 reduce-scatter.1
  743.2 92.8 all-gather.2
where the time goes:
time: 856 us; the launch traced here: 855 us
  waiting for transfers between devices  718 us (84%)
  blocking collectives  68.6 us (8%)
  other arithmetic  28.4 us (3%)
  between operations  15.7 us (2%)
  matrix products  12.7 us (1%)
  local copies, waits for them, and re-layouts  11.2 us (1%)
    reduce_scatter x1, waiting for transfers between devices, shards(): lax.psum_scatter(forward_part(facet_data, x_begin, every_spot, forward_ta...  626 us
    all_gather x1, waiting for transfers between devices, shards(): lax.all_gather(regridded_values, ('facet', 'sub'), axis=0, tiled=True)  92.4 us
    unnamed x1, blocking collectives  68.6 us
  transfers between devices with their start and end apart: 2, of which 2 were waited for; matrix products, arithmetic and copies ran while one was open for 0% of the time, Pallas kernels for 0%

commit v1 on v0

v1 whole, which is shorter than its diff:
```python
import math

import jax
import jax.numpy as jnp
import numpy as np
from jax import lax
from jax.sharding import PartitionSpec as P

SG = 512
KS = 8
OVER = 16
RES = 128
BF = jnp.bfloat16
F32 = jnp.float32


def split(value):
    high = lax.reduce_precision(value, 8, 7)
    return high.astype(BF), (value - high).astype(BF)


def complex_rows(cos_part, sin_part):
    return jnp.concatenate(
        [
            jnp.concatenate([cos_part, sin_part], 1),
            jnp.concatenate([-sin_part, cos_part], 1),
        ],
        0,
    )


def gather_by_exchange(value, axis):
    count = lax.axis_size(axis)
    copies = jnp.broadcast_to(value[None], (count,) + value.shape)
    return lax.all_to_all(copies, axis, 0, 0, tiled=True)


def angle_table(rows, columns, period):
    turn = (rows[:, None] * columns[None, :]) % period
    angle = turn.astype(F32) * (2.0 * math.pi / period)
    return jnp.cos(angle), jnp.sin(angle)


def weights(fine_index, cells):
    cell = fine_index // OVER
    frac = fine_index % OVER
    offset = jnp.arange(cells, dtype=jnp.int32)[None, :, None] - cell[:, None, :]
    distance = offset.astype(F32) - (KS - 1) / 2.0 - frac.astype(F32)[:, None, :] / OVER
    weight = jnp.exp(-0.5 * (distance / 0.6) ** 2)
    return jnp.where((offset >= 0) & (offset < KS), weight, F32(0.0))


def shards(facet_data, subgrid_pos, vis_counts, vis_u_fine, vis_v_fine, vis_observed):
    facets = lax.axis_size("facet")
    subs = lax.axis_size("sub")
    rows_v = facet_data.shape[1]
    slots = vis_u_fine.shape[1]
    facet = lax.axis_index("facet")
    inside = jnp.arange(SG, dtype=jnp.int32)
    residue = jnp.arange(RES, dtype=jnp.int32)

    gathered = gather_by_exchange(facet_data, "sub")

    ends = jnp.concatenate([subgrid_pos // RES, vis_counts]).astype(F32)
    meta = jnp.stack(
        [
            vis_u_fine[0].astype(F32),
            vis_v_fine[0].astype(F32),
            vis_observed[0, 0],
            vis_observed[1, 0],
            jnp.pad(ends, (0, slots - 2)),
        ]
    )
    meta = gather_by_exchange(meta, "facet")
    u_fine = meta[:, 0].astype(jnp.int32)
    v_fine = meta[:, 1].astype(jnp.int32)
    observed = meta[:, 2:4]
    spot = meta[:, 4, 0].astype(jnp.int32)
    counts = meta[:, 4, 1].astype(jnp.int32)

    weight_u = weights(u_fine, SG).astype(BF)
    weight_v = weights(v_fine, rows_v)

    blocks = facet * subs + jnp.arange(subs, dtype=jnp.int32)
    cos_d, sin_d = angle_table(residue, blocks, RES)
    high_d, low_d = split(complex_rows(cos_d, sin_d))
    turn = (residue[:, None] * inside[None, :]).astype(F32) * (2.0 * math.pi / 65536)
    tw_cos, tw_sin = jnp.cos(turn)[:, None, :], jnp.sin(turn)[:, None, :]
    lines = (spot[:, None] + jnp.arange(4, dtype=jnp.int32)[None, :]).reshape(-1)
    cos_e, sin_e = angle_table(lines, inside, SG)
    high_e, low_e = split(complex_rows(cos_e, sin_e) * F32(1.0 / 256.0))

    stack = jnp.moveaxis(gathered, 1, 0).reshape(2 * subs, rows_v, SG)
    spread = jnp.einsum("aj,jvx->avx", high_d, stack, preferred_element_type=F32)
    spread = spread + jnp.einsum("aj,jvx->avx", low_d, stack, preferred_element_type=F32)
    real_g, imag_g = spread[:RES], spread[RES:]
    real_h = (real_g * tw_cos + imag_g * tw_sin).astype(BF)
    imag_h = (imag_g * tw_cos - real_g * tw_sin).astype(BF)
    both = jnp.concatenate([real_h, imag_h], -1)
    share = jnp.einsum("rx,fvx->rvf", high_e, both, preferred_element_type=F32)
    share = share + jnp.einsum("rx,fvx->rvf", low_e, both, preferred_element_type=F32)
    share = share.reshape(2, facets, 4, rows_v, RES).transpose(1, 0, 3, 2, 4)
    share = share.reshape(facets, 2, rows_v, SG).astype(BF)
    along = jnp.einsum("scvu,suk->scvk", share, weight_u, preferred_element_type=F32)
    part = jnp.sum(along * weight_v[:, None], 2)

    predicted = jnp.sum(gather_by_exchange(part, "facet"), 0)

    live = inside[None, None, :slots] < counts[:, None, None]
    residual = jnp.where(live, observed - predicted, F32(0.0))
    mine = lax.dynamic_index_in_dim(residual, facet, 0, keepdims=False)[:, None]

    spreaded = (residual[:, :, None] * weight_v[:, None]).astype(BF)
    regrid = jnp.einsum("scvk,suk->scvu", spreaded, weight_u, preferred_element_type=F32)
    regrid = regrid.astype(BF).reshape(facets, 2, rows_v, 4, RES)
    regrid = regrid.transpose(1, 0, 3, 2, 4).reshape(8 * facets, rows_v, RES)
    back = jnp.einsum("rx,rvf->fvx", high_e, regrid, preferred_element_type=F32)
    back = back + jnp.einsum("rx,rvf->fvx", low_e, regrid, preferred_element_type=F32)
    real_b, imag_b = back[..., :SG], back[..., SG:]
    real_m = (real_b * tw_cos - imag_b * tw_sin).astype(BF)
    imag_m = (imag_b * tw_cos + real_b * tw_sin).astype(BF)
    stacked = jnp.concatenate([real_m, imag_m], 0)
    image = jnp.einsum("aj,avx->jvx", high_d, stacked, preferred_element_type=F32)
    image = image + jnp.einsum("aj,avx->jvx", low_d, stacked, preferred_element_type=F32)
    image = image.reshape(2, subs, rows_v, SG).transpose(1, 0, 2, 3).astype(BF)
    image = lax.all_to_all(image, "sub", 0, 0, tiled=True)
    return (mine, jnp.sum(image.astype(F32), 0))


def solution(mesh):
    return jax.shard_map(
        shards,
        mesh=mesh,
        in_specs=(
            P(None, None, ("facet", "sub")),
            P(("facet", "sub")),
            P(("facet", "sub")),
            P(("facet", "sub"), None),
            P(("facet", "sub"), None),
            P(None, ("facet", "sub"), None),
        ),
        out_specs=(P(None, ("facet", "sub"), None), P(None, None, ("facet", "sub"))),
        check_vma=False,
    )
```

time: 856 us -> 86.2 us (0.10)
  waiting for transfers between devices: 718 us -> 28.8 us
  blocking collectives: 68.6 us -> 0 us
  starting transfers between devices: 0.08 us -> 22.4 us
  other arithmetic: 28.4 us -> 7.31 us
  between operations: 15.7 us -> 2.15 us
    reduce_scatter x1 -> x0, waiting for transfers between devices: 626 us -> none  [shards(): lax.psum_scatter(forward_part(facet_data, x_begin, every_spot, forward_ta...]
    all_gather x1 -> x0, waiting for transfers between devices: 92.4 us -> none  [shards(): lax.all_gather(regridded_values, ('facet', 'sub'), axis=0, tiled=True)]
    unnamed x1 -> x0, blocking collectives: 68.6 us -> none
    all_to_all x0 -> x4, waiting for transfers between devices: none -> 28.8 us  [the longest x3 18.9 us: gather_by_exchange(): return lax.all_to_all(copies, axis, 0, 0, tiled=True)]
    all_to_all x0 -> x4, starting transfers between devices: none -> 22.4 us  [the longest x3 18.8 us: gather_by_exchange(): return lax.all_to_all(copies, axis, 0, 0, tiled=True)]
    dot_general x4 -> x10, matrix products: 12.7 us -> 17.5 us  [the longest x1 4.06 us: shards(): jnp.einsum('scvu,suk->scvk', share, weight_u, preferred_element_type=F32)]
  transfers between devices with their start and end apart: 2 -> 4, of which waited for: 2 -> 4; matrix products, arithmetic and copies ran while one was open for 0% -> 5% of each run, Pallas kernels for 0% -> 0%
where the time goes in v1:
time: 86.2 us; the launch traced here: 84.9 us
  waiting for transfers between devices  28.8 us (33%)
  starting transfers between devices  22.4 us (26%)
  matrix products  17.5 us (20%)
  other arithmetic  7.31 us (8%)
  local copies, waits for them, and re-layouts  6.77 us (8%)
  between operations  2.15 us (2%)
    all_to_all x3, waiting for transfers between devices, gather_by_exchange(): return lax.all_to_all(copies, axis, 0, 0, tiled=True)  18.9 us
    all_to_all x3, starting transfers between devices, gather_by_exchange(): return lax.all_to_all(copies, axis, 0, 0, tiled=True)  18.8 us
    all_to_all x1, waiting for transfers between devices, shards(): image = lax.all_to_all(image, 'sub', 0, 0, tiled=True)  9.88 us
    dot_general x1, matrix products, shards(): jnp.einsum('scvu,suk->scvk', share, weight_u, preferred_element_type=F32)  4.06 us
    dot_general x1, matrix products, shards(): jnp.einsum('scvk,suk->scvu', spreaded, weight_u, preferred_element_type=F32)  3.9 us
    all_to_all x1, starting transfers between devices, shards(): image = lax.all_to_all(image, 'sub', 0, 0, tiled=True)  3.57 us
    broadcast_in_dim x3, local copies, waits for them, and re-layouts, gather_by_exchange(): copies = jnp.broadcast_to(value[None], (count,) + value.shape)  2.57 us
  transfers between devices with their start and end apart: 4, of which 4 were waited for; matrix products, arithmetic and copies ran while one was open for 5% of the time, Pallas kernels for 0%

profile of v1, /device:TPU:1, one launch (start us, length us, event | category | flops | bytes accessed | tf_op | source)
XLA Modules:
  0.0 84.9 jit_solution(17027080219290753635)
XLA Ops:
  4.8 6.0 %all-to-all-start = ((f32[8,5,512]{2,1,0:T(8,128)}), f32[8,5,512]{2,1,0:T(8,128)S(1)}, u32[]{:S(2)}, u32[]{:S(2)}) async-start(f32[8,5,512]{2,1,0:T(8,128)} %broadcast_in_dim.24), calls=%async_computation | async-start | bytes 262144 | tf_op jit(solution)/shard_map/all_to_all | solution.py:35
  10.8 0.8 copy.53
  11.7 0.9 %fusion.35 = (f32[128,512]{1,0:T(8,128)S(1)}, f32[128,512]{1,0:T(8,128)S(1)}) fusion(), kind=kLoop, calls=%fused_computation.46 | loop fusion | flops 196608 | bytes 524288 | tf_op jit(solution)/shard_map/sin | solution.py:88
  12.6 3.4 %all-to-all-done = f32[8,5,512]{2,1,0:T(8,128)S(1)} async-done(((f32[8,5,512]{2,1,0:T(8,128)}), f32[8,5,512]{2,1,0:T(8,128)S(1)}, u32[]{:S(2)}, u32[]{:S(2)}) %all-to-all-start) | async-done | bytes 81952 | tf_op jit(solution)/shard_map/all_to_all | solution.py:35
  16.0 1.2 %broadcast_in_dim.26 = bf16[16,2,16,512]{3,1,2,0:T(2,128)(2,1)} broadcast(bf16[2,16,512]{2,0,1:T(2,128)(2,1)S(1)} %copy.53), dimensions={1,2,3} | broadcast | bytes 557056 | tf_op jit(solution)/shard_map/broadcast_in_dim | solution.py:34
  17.2 7.6 %all-to-all-start.1 = ((bf16[16,2,16,512]{3,1,2,0:T(2,128)(2,1)}), bf16[16,2,16,512]{3,1,2,0:T(2,128)(2,1)S(1)}, u32[]{:S(2)}, u32[]{:S(2)}) async-start(bf16[16,2,16,512]{3,1,2,0:T(2,128)(2,1)} %broadcast_in_dim.26), calls=%async_computation.1 | async-start | bytes 1048576 | tf_op jit(solution)/shard_map/all_to_all | solution.py:35
  26.2 9.2 %all-to-all-done.1 = bf16[16,2,16,512]{3,1,2,0:T(2,128)(2,1)S(1)} async-done(((bf16[16,2,16,512]{3,1,2,0:T(2,128)(2,1)}), bf16[16,2,16,512]{3,1,2,0:T(2,128)(2,1)S(1)}, u32[]{:S(2)}, u32[]{:S(2)}) %all-to-all-start.1) | async-done | bytes 524320 | tf_op jit(solution)/shard_map/all_to_all | solution.py:35
  35.6 1.3 %fusion.68 = f32[256,16,512]{2,0,1:T(8,128)S(1)} fusion(bf16[32,16,512]{2,0,1:T(8,128)(2,1)S(1)} %bitcast.71, f32[128,16]{0,1:T(8,128)S(1)} %get-tuple-element.33, f32[128,16]{0,1:T(8,128)S(1)} %get-tuple-element.32, f32[128,16]{0,1:T(8,128)S(1)} %get-tuple-element.31), kind=kOutput, calls=%fused_computation.105 | convolution fusion | flops 134258688 | bytes 8937472 | tf_op jit(solution)/shard_map/aj,jvx->avx/dot_general | solution.py:94
  36.9 1.3 %convolution_add_fusion = f32[256,16,512]{2,0,1:T(8,128)S(1)} fusion(f32[256,16,512]{2,0,1:T(8,128)S(1)} %fusion.68, bf16[32,16,512]{2,0,1:T(8,128)(2,1)S(1)} %bitcast.72, f32[128,16]{0,1:T(8,128)S(1)} %get-tuple-element.33, f32[128,16]{0,1:T(8,128)S(1)} %get-tuple-element.32, f32[128,16]{0,1:T(8,128)S(1)} %get-tuple-element.31), kind=kOutput, calls=%fused_computation.19 | convolution fusion | flops 136364032 | bytes 17326080 | tf_op jit(solution)/shard_map/aj,jvx->avx/dot_general | solution.py:95
  38.2 1.4 %add_convert_fusion.1 = (bf16[128,16,512]{2,0,1:T(8,128)(2,1)S(1)}, bf16[128,16,512]{2,0,1:T(8,128)(2,1)S(1)}) fusion(f32[256,16,512]{2,0,1:T(8,128)S(1)} %convolution_add_fusion, f32[128,512]{1,0:T(8,128)S(1)} %get-tuple-element.38, f32[128,512]{1,0:T(8,128)S(1)} %get-tuple-element.39), kind=kLoop, calls=%fused_computation.18 | loop fusion | flops 8388608 | bytes 13107200 | tf_op jit(solution)/shard_map/convert_element_type | solution.py:97
  39.6 1.4 %fusion.14 = f32[128,16,64]{0,2,1:T(8,128)S(1)} fusion(bf16[128,16,512]{2,0,1:T(8,128)(2,1)S(1)} %get-tuple-element.23, bf16[128,16,512]{2,0,1:T(8,128)(2,1)S(1)} %get-tuple-element.22, f32[32,512]{1,0:T(8,128)S(1)} %get-tuple-element.30, f32[32,512]{1,0:T(8,128)S(1)} %get-tuple-element.29, f32[32,512]{1,0:T(8,128)S(1)} %get-tuple-element.28), kind=kOutput, calls=%fused_computation.22 | convolution fusion | flops 277282816 | bytes 4915200 | tf_op jit(solution)/shard_map/rx,fvx->rvf/dot_general | solution.py:101
  41.0 1.4 %fusion.22 = bf16[128,16,64]{0,2,1:T(8,128)(2,1)S(1)} fusion(f32[128,16,64]{0,2,1:T(8,128)S(1)} %fusion.14, bf16[128,16,512]{2,0,1:T(8,128)(2,1)S(1)} %get-tuple-element.23, bf16[128,16,512]{2,0,1:T(8,128)(2,1)S(1)} %get-tuple-element.22, f32[32,512]{1,0:T(8,128)S(1)} %get-tuple-element.30, f32[32,512]{1,0:T(8,128)S(1)} %get-tuple-element.29, ...), kind=kOutput, calls=%fused_computation.28 | convolution fusion | flops 277479424 | bytes 5177344 | tf_op jit(solution)/shard_map/rx,fvx->rvf/dot_general | solution.py:100
  42.5 4.1 %fusion.26 = f32[8,2,512]{2,1,0:T(2,128)S(1)} fusion(f32[8,512]{1,0:T(8,128)S(1)} %bitcast.80, s32[8,512]{1,0:T(8,128)S(1)} %get-tuple-element.37, bf16[8,2,16,512]{3,0,1,2:T(8,128)(2,1)S(1)} %reshape.122, f32[8,16,512]{2,1,0:T(8,128)S(1)} %exponential_select_fusion), kind=kOutput, calls=%fused_computation.30 | convolution fusion | flops 159637504 | bytes 589824 | tf_op jit(solution)/shard_map/scvu,suk->scvk/dot_general | solution.py:104
  47.3 5.3 %all-to-all-start.2 = ((f32[8,8,2,512]{3,1,2,0:T(8,128)}), f32[8,8,2,512]{3,1,2,0:T(8,128)S(1)}, u32[]{:S(2)}, u32[]{:S(2)}) async-start(f32[8,8,2,512]{3,1,2,0:T(8,128)} %broadcast_in_dim.29), calls=%async_computation.2 | async-start | bytes 524288 | tf_op jit(solution)/shard_map/all_to_all | solution.py:35
  52.7 6.4 %all-to-all-done.2 = f32[8,8,2,512]{3,1,2,0:T(8,128)S(1)} async-done(((f32[8,8,2,512]{3,1,2,0:T(8,128)}), f32[8,8,2,512]{3,1,2,0:T(8,128)S(1)}, u32[]{:S(2)}, u32[]{:S(2)}) %all-to-all-start.2) | async-done | bytes 262176 | tf_op jit(solution)/shard_map/all_to_all | solution.py:35
  59.2 3.9 %fusion.23 = bf16[8,2,16,512]{3,2,1,0:T(8,128)(2,1)S(1)} fusion(f32[8,512]{1,0:T(8,128)S(1)} %bitcast.81, s32[8,512]{1,0:T(8,128)S(1)} %get-tuple-element.37, f32[8,2,512]{2,1,0:T(2,128)S(1)} %copy.57, f32[8,16,512]{2,1,0:T(8,128)S(1)} %exponential_select_fusion), kind=kOutput, calls=%fused_computation.29 | convolution fusion | flops 159776768 | bytes 589824 | tf_op jit(solution)/shard_map/scvk,suk->scvu/dot_general | solution.py:114
  63.3 1.3 %fusion.40 = f32[16,128,1024]{2,1,0:T(8,128)S(1)} fusion(bf16[64,16,128]{2,0,1:T(8,128)(2,1)S(1)} %bitcast.73, f32[32,512]{1,0:T(8,128)S(1)} %get-tuple-element.30, f32[32,512]{1,0:T(8,128)S(1)} %get-tuple-element.29, f32[32,512]{1,0:T(8,128)S(1)} %get-tuple-element.28), kind=kOutput, calls=%fused_computation.51 | convolution fusion | flops 268828672 | bytes 8847360 | tf_op jit(solution)/shard_map/rx,rvf->fvx/dot_general | solution.py:117
  64.5 1.3 %add_bitcast_fusion = f32[128,16,1024]{2,0,1:T(8,128)S(1)} fusion(f32[16,128,1024]{2,1,0:T(8,128)S(1)} %fusion.40, bf16[64,16,128]{2,0,1:T(8,128)(2,1)S(1)} %bitcast.74, f32[32,512]{1,0:T(8,128)S(1)} %get-tuple-element.30, f32[32,512]{1,0:T(8,128)S(1)} %get-tuple-element.29, f32[32,512]{1,0:T(8,128)S(1)} %get-tuple-element.28), kind=kOutput, calls=%fused_computation | convolution fusion | flops 270991360 | bytes 17235968 | tf_op jit(solution)/shard_map/rx,rvf->fvx/dot_general | solution.py:118
  65.8 1.4 %subtract_convert_fusion = (bf16[128,16,512]{2,0,1:T(8,128)(2,1)S(1)}, bf16[128,16,512]{2,0,1:T(8,128)(2,1)S(1)}) fusion(f32[128,16,1024]{2,0,1:T(8,128)S(1)} %add_bitcast_fusion, f32[128,512]{1,0:T(8,128)S(1)} %get-tuple-element.38, f32[128,512]{1,0:T(8,128)S(1)} %get-tuple-element.39), kind=kLoop, calls=%fused_computation.10 | loop fusion | flops 8388608 | bytes 13107200 | tf_op jit(solution)/shard_map/convert_element_type | solution.py:120
  67.2 0.8 fusion.12
  68.0 0.8 fusion.17
  68.8 1.3 %copy.83 = bf16[2,16,16,512]{3,0,2,1:T(2,128)(2,1)} copy(bf16[2,16,16,512]{3,1,0,2:T(8,128)(2,1)S(1)} %bitcast.77) | data formatting | bytes 1048576 | tf_op jit(solution)/shard_map/convert_element_type | solution.py:125
  70.2 3.6 %all-to-all-start.3 = ((bf16[16,2,16,512]{3,1,2,0:T(2,128)(2,1)}), bf16[16,2,16,512]{3,1,2,0:T(2,128)(2,1)S(1)}, u32[]{:S(2)}, u32[]{:S(2)}) async-start(bf16[16,2,16,512]{3,1,2,0:T(2,128)(2,1)} %bitcast.68), calls=%async_computation.3 | async-start | bytes 1048576 | tf_op jit(solution)/shard_map/all_to_all | solution.py:126
  74.4 9.9 %all-to-all-done.3 = bf16[16,2,16,512]{3,1,2,0:T(2,128)(2,1)S(1)} async-done(((bf16[16,2,16,512]{3,1,2,0:T(2,128)(2,1)}), bf16[16,2,16,512]{3,1,2,0:T(2,128)(2,1)S(1)}, u32[]{:S(2)}, u32[]{:S(2)}) %all-to-all-start.3) | async-done | bytes 524320 | tf_op jit(solution)/shard_map/all_to_all | solution.py:126
  (32 shorter events, 7.0 us)
Async XLA Ops:
  4.8 11.2 %all-to-all-start = ((f32[8,5,512]{2,1,0:T(8,128)}), f32[8,5,512]{2,1,0:T(8,128)S(1)}, u32[]{:S(2)}, u32[]{:S(2)}) async-start(f32[8,5,512]{2,1,0:T(8,128)} %broadcast_in_dim.24), calls=%async_computation | async-start | bytes 262144 | tf_op jit(solution)/shard_map/all_to_all | solution.py:35
  17.2 18.1 %all-to-all-start.1 = ((bf16[16,2,16,512]{3,1,2,0:T(2,128)(2,1)}), bf16[16,2,16,512]{3,1,2,0:T(2,128)(2,1)S(1)}, u32[]{:S(2)}, u32[]{:S(2)}) async-start(bf16[16,2,16,512]{3,1,2,0:T(2,128)(2,1)} %broadcast_in_dim.26), calls=%async_computation.1 | async-start | bytes 1048576 | tf_op jit(solution)/shard_map/all_to_all | solution.py:35
  47.3 11.8 %all-to-all-start.2 = ((f32[8,8,2,512]{3,1,2,0:T(8,128)}), f32[8,8,2,512]{3,1,2,0:T(8,128)S(1)}, u32[]{:S(2)}, u32[]{:S(2)}) async-start(f32[8,8,2,512]{3,1,2,0:T(8,128)} %broadcast_in_dim.29), calls=%async_computation.2 | async-start | bytes 524288 | tf_op jit(solution)/shard_map/all_to_all | solution.py:35
  70.2 14.1 %all-to-all-start.3 = ((bf16[16,2,16,512]{3,1,2,0:T(2,128)(2,1)}), bf16[16,2,16,512]{3,1,2,0:T(2,128)(2,1)S(1)}, u32[]{:S(2)}, u32[]{:S(2)}) async-start(bf16[16,2,16,512]{3,1,2,0:T(2,128)(2,1)} %bitcast.68), calls=%async_computation.3 | async-start | bytes 1048576 | tf_op jit(solution)/shard_map/all_to_all | solution.py:126
